TPU v7x, 256 devices: a whole 4x4x8 slice. The times are simulated.
256 devices in a mesh: row: 16 (over x_hi, z), blk: 16 (over x_lo, y, core).
Axes of the slice: x: 4 (x_hi: 2, x_lo: 2; x = x_hi * 2 + x_lo), y: 4, z: 8, core: 2. Of those that a mesh axis runs over, the one named last changes fastest.
Arguments:
- source_table: bfloat16 [8192, 512], P('blk'), may hold values from -6 to 6
- target_table: bfloat16 [131072, 512], P(('row', 'blk')), may hold values from -6 to 6
- message_weight: bfloat16 [512, 512], replicated, may hold values from -0.25 to 0.25
- self_weight: bfloat16 [512, 512], replicated, may hold values from -0.25 to 0.25
- tile_lists: int32 [256, 16], P(('row', 'blk')), may hold values from 0 to 15, each once within a row
- key_offsets: int32 [131072, 16], P(('row', 'blk')), may hold values from 0 to 511
- list_lengths: int32 [256], P(('row', 'blk')), may hold values from 1 to 16, 2048 in all
- cotangent: bfloat16 [131072, 512], P(('row', 'blk')), may hold values from -6 to 6
Outputs:
- updated: bfloat16 [131072, 512], P(('row', 'blk'))
- target_gradient: bfloat16 [131072, 512], P(('row', 'blk'))
- source_gradient: bfloat16 [8192, 512], P(('blk', 'row'))
- self_gradient: float32 [512, 512], replicated
- message_gradient: float32 [512, 512], replicated
Inputs may be any that keep to these rules, and one draw needn't show every extreme that they name: Each row of tile_lists names every one of the 16 source tiles once. A target tile uses the first list_lengths entries of its row of tile_lists.
All inputs are finite; a program needn't handle non-finite values. No bound on the sum of `list_lengths` on one device may be relied on, other than what follows from the above.
Results may differ from a plain program's by a relative error of at most 0.0058.
Values may be sent and summed in bfloat16 or wider, within the bound.
A program may use at most 64 MiB of HBM per device.

v0:
```python
import jax
import jax.numpy as jnp
from jax import lax
from jax.sharding import PartitionSpec as P


def slot_table(lists):
    slot_count = lists.shape[1]
    slot_ids = lax.iota(jnp.int32, slot_count)
    matches = lists[:, :, None] == slot_ids[None, None, :]
    return jnp.sum(jnp.where(matches, slot_ids[None, :, None], 0), axis=1)


def tile_patterns(offset_tiles, slot_column, lengths, tile_rows):
    slot_count = offset_tiles.shape[2]
    chosen_slot = lax.iota(jnp.int32, slot_count)[None, None, :] == slot_column[:, None, None]
    chosen = jnp.sum(jnp.where(chosen_slot, offset_tiles, 0), axis=2)
    used = slot_column < lengths
    positions = lax.iota(jnp.int32, tile_rows)
    pattern = (chosen[:, :, None] == positions[None, None, :]) & used[:, None, None]
    return pattern.astype(jnp.bfloat16)


def local(
    source_table,
    target_table,
    message_weight,
    self_weight,
    tile_lists,
    key_offsets,
    list_lengths,
    cotangent,
):
    tile_rows = target_table.shape[0] // tile_lists.shape[0]
    tiles_here = tile_lists.shape[0]
    slot_count = tile_lists.shape[1]
    width = target_table.shape[1]
    block_rows = source_table.shape[0]
    row_devices = lax.axis_size("row")
    share_rows = block_rows // row_devices
    own_rows = lax.dynamic_slice_in_dim(
        source_table, lax.axis_index("row") * share_rows, share_rows, 0
    )
    projected = jnp.dot(source_table, message_weight, preferred_element_type=jnp.float32).astype(
        jnp.bfloat16
    )
    inverse_tile = 1.0 / list_lengths.astype(jnp.float32)
    slot_of = slot_table(tile_lists)
    offset_tiles = key_offsets.reshape(tiles_here, tile_rows, slot_count)
    start_sum = jnp.zeros((target_table.shape[0], width), jnp.float32)
    pieces = lax.all_gather(projected, "blk", axis=0, tiled=True)
    piece_tiles = pieces.shape[0] // tile_rows

    def gather_visit(local_tile, running):
        source_tile = lax.dynamic_slice_in_dim(pieces, local_tile * tile_rows, tile_rows, 0)
        slot_column = lax.dynamic_index_in_dim(slot_of, local_tile, 1, keepdims=False)
        pattern = tile_patterns(offset_tiles, slot_column, list_lengths, tile_rows)
        added = jnp.einsum("trc,cw->trw", pattern, source_tile, preferred_element_type=jnp.float32)
        return running + added.reshape(running.shape)

    gathered = lax.fori_loop(0, piece_tiles, gather_visit, start_sum)
    inverse_row = jnp.repeat(inverse_tile, tile_rows)[:, None]
    preact = (
        jnp.dot(target_table, self_weight, preferred_element_type=jnp.float32)
        + gathered * inverse_row
    )
    sigmoid_pre = jax.nn.sigmoid(preact)
    updated = (target_table.astype(jnp.float32) + preact * sigmoid_pre).astype(jnp.bfloat16)
    upstream = cotangent.astype(jnp.float32)
    grad_pre = (upstream * sigmoid_pre * (1.0 + preact * (1.0 - sigmoid_pre))).astype(jnp.bfloat16)
    target_gradient = (
        upstream + jnp.dot(grad_pre, self_weight.T, preferred_element_type=jnp.float32)
    ).astype(jnp.bfloat16)
    grad_tiles = grad_pre.reshape(tiles_here, tile_rows, width)

    def tile_terms(slot_column, offsets, lengths, inverses, grads):
        pattern = tile_patterns(offsets, slot_column, lengths, tile_rows)
        terms = jnp.einsum("trc,trw->tcw", pattern, grads, preferred_element_type=jnp.float32)
        return jnp.sum(terms * inverses[:, None, None], axis=0)

    def partial_visit(local_tile, running):
        slot_column = lax.dynamic_index_in_dim(slot_of, local_tile, 1, keepdims=False)
        term = tile_terms(slot_column, offset_tiles, list_lengths, inverse_tile, grad_tiles)
        return lax.dynamic_update_slice_in_dim(running, term, local_tile * tile_rows, 0)

    block_sum = lax.psum_scatter(
        lax.fori_loop(
            0,
            block_rows * lax.axis_size("blk") // tile_rows,
            partial_visit,
            jnp.zeros((block_rows * lax.axis_size("blk"), width), jnp.float32),
        ),
        "blk",
        scatter_dimension=0,
        tiled=True,
    )
    source_sum = lax.psum_scatter(block_sum, "row", scatter_dimension=0, tiled=True)
    source_grad_rounded = source_sum.astype(jnp.bfloat16)
    source_gradient = jnp.dot(
        source_grad_rounded, message_weight.T, preferred_element_type=jnp.float32
    ).astype(jnp.bfloat16)
    self_partial = jnp.dot(target_table.T, grad_pre, preferred_element_type=jnp.float32)
    message_partial = jnp.dot(own_rows.T, source_grad_rounded, preferred_element_type=jnp.float32)
    self_total, message_total = lax.psum((self_partial, message_partial), ("row", "blk"))
    target_total = target_table.shape[0] * row_devices * lax.axis_size("blk")
    source_total = block_rows * lax.axis_size("blk")
    self_gradient = self_total * target_total ** (-0.5)
    message_gradient = message_total * source_total ** (-0.5)
    return (updated, target_gradient, source_gradient, self_gradient, message_gradient)


def solution(mesh):
    placed = (
        P("blk", None),
        P(("row", "blk"), None),
        P(),
        P(),
        P(("row", "blk"), None),
        P(("row", "blk"), None),
        P(("row", "blk")),
        P(("row", "blk"), None),
    )
    return jax.shard_map(
        local,
        mesh=mesh,
        in_specs=placed,
        out_specs=(
            P(("row", "blk"), None),
            P(("row", "blk"), None),
            P(("blk", "row"), None),
            P(),
            P(),
        ),
        check_vma=False,
    )
```

profile of v0, /device:TPU:2, one launch (start us, length us, event | category | flops | bytes accessed | tf_op | source)
XLA Modules:
  0.0 807.8 jit_solution(3190670035176118978)
XLA Ops:
  7.2 2.5 convolution_convert_fusion
  11.2 56.8 %all-gather.2.cloned.1.call-done = bf16[8192,512]{1,0:T(8,128)(2,1)} async-done(((bf16[512,512]{1,0:T(8,128)(2,1)}), bf16[8192,512]{1,0:T(8,128)(2,1)}) %all-gather.2.cloned.1.call-update) | async-done | bytes 8388624 | tf_op jit(solution)/shard_map/all_gather | solution.py:51
  68.0 80.6 %while.28 = (s32[]{:T(128)}, f32[512,512]{1,0:T(8,128)S(1)}, s32[1,16]{1,0:T(1,128)S(1)}, s32[1,512,16]{1,2,0:T(8,128)}, s32[1]{0:T(128)}, /*index=5*/bf16[8192,...) while((s32[]{:T(128)}, f32[512,512]{1,0:T(8,128)S(1)}, s32[1,16]{1,0:T(1,128)S(1)}, ...), condition=%wide.region_3.4_spmd.clone, body=%wide.region_1.3_spmd.clone.sunk | while | flops 269499936 | bytes 2659034 | solution.py:61
  71.4 1.6 convolution_add_fusion.4
  76.4 1.6 convolution_add_fusion.4
  81.5 1.6 convolution_add_fusion.4
  86.5 1.6 convolution_add_fusion.4
  91.6 1.6 convolution_add_fusion.4
  96.6 1.6 convolution_add_fusion.4
  101.6 1.6 convolution_add_fusion.4
  106.7 1.6 convolution_add_fusion.4
  111.7 1.6 convolution_add_fusion.4
  116.8 1.6 convolution_add_fusion.4
  121.8 1.6 convolution_add_fusion.4
  126.8 1.6 convolution_add_fusion.4
  131.9 1.6 convolution_add_fusion.4
  136.9 1.6 convolution_add_fusion.4
  142.0 1.6 convolution_add_fusion.4
  147.0 1.6 convolution_add_fusion.4
  148.7 3.0 fusion.15
  151.7 7.9 broadcast_in_dim.94
  159.6 67.2 %while.27 = (s32[]{:T(128)}, f32[8192,512]{1,0:T(8,128)}, s32[1,16]{1,0:T(1,128)S(1)}, s32[1,512,16]{1,2,0:T(8,128)S(1)}, s32[1]{0:T(128)}, /*index=5*/bf16[1,51...) while((s32[]{:T(128)}, f32[8192,512]{1,0:T(8,128)}, ...), condition=%wide.region_6.7_spmd, body=%wide.region_4.6_spmd.sunk | while | flops 269237792 | bytes 1610968 | solution.py:87
  166.4 1.6 fusion.37
  183.2 1.6 fusion.37
  195.8 1.6 fusion.37
  212.6 1.6 fusion.37
  226.8 101.1 %reduce-scatter.3.cloned.1.call-done = f32[512,512]{1,0:T(8,128)} async-done(((f32[8192,512]{1,0:T(8,128)}), f32[512,512]{1,0:T(8,128)}) %reduce-scatter.3.cloned.1.call-update) | async-done | bytes 1048592 | tf_op jit(solution)/shard_map/reduce_scatter | solution.py:86
  329.4 200.2 %reduce-scatter.5.cloned.1.call-done = f32[32,512]{1,0:T(8,128)} async-done(((f32[512,512]{1,0:T(8,128)}), f32[32,512]{1,0:T(8,128)}) %reduce-scatter.5.cloned.1.call-update) | async-done | bytes 65552 | tf_op jit(solution)/shard_map/reduce_scatter | solution.py:97
  529.6 2.1 fusion.16
  533.1 1.7 convolution_convert_fusion.1
  534.8 261.5 %all-reduce.3.cloned.1.call-done = (f32[512,512]{0,1:T(8,128)}, f32[512,512]{1,0:T(8,128)}) async-done(((f32[512,512]{0,1:T(8,128)}, f32[512,512]{1,0:T(8,128)}), (f32[512,512]{0,1:T(8,128)}, f32[512,512]{1,0:T(8,128)})) %all-reduce.3.cloned.1.call-update) | async-done | bytes 2097168 | tf_op jit(solution)/shard_map/psum | solution.py:104
  799.0 2.3 broadcast_multiply_fusion
  (132 shorter events, 79.4 us)
Async XLA Ops:
  7.2 141.5 %copy-start = (bf16[512,512]{1,0:T(8,128)(2,1)S(1)}, bf16[512,512]{1,0:T(8,128)(2,1)}, u32[]{:S(2)}) copy-start(bf16[512,512]{1,0:T(8,128)(2,1)} %param.15) | copy-start | bytes 1572868
  7.2 60.8 %all-gather.2.cloned.1.call-start = ((), (), s32[]{:S(2)}) async-start(), calls=%async_computation.2 | async-start | bytes 8912896 | tf_op jit(solution)/shard_map/all_gather | solution.py:51
  9.7 318.2 %reduce-scatter.3.cloned.1.call-start = ((), (), s32[]{:S(2)}) async-start(), calls=%async_computation.3 | async-start | bytes 17825792 | tf_op jit(solution)/shard_map/reduce_scatter | solution.py:86
  148.6 10.9 %copy-start.1 = (s32[1,512,16]{1,2,0:T(8,128)S(1)}, s32[1,512,16]{1,2,0:T(8,128)}, u32[]{:S(2)}) copy-start(s32[1,512,16]{1,2,0:T(8,128)} %get-tuple-element.461) | copy-start | bytes 98308
  159.6 168.4 %copy-start.3 = (bf16[512,512]{1,0:T(8,128)(2,1)S(1)}, bf16[512,512]{1,0:T(8,128)(2,1)}, u32[]{:S(2)}) copy-start(bf16[512,512]{1,0:T(8,128)(2,1)} %param.13) | copy-start | bytes 1572868
  159.6 372.2 %copy-start.4 = (bf16[512,512]{1,0:T(8,128)(2,1)S(1)}, bf16[512,512]{1,0:T(8,128)(2,1)}, u32[]{:S(2)}) copy-start(bf16[512,512]{1,0:T(8,128)(2,1)} %param.19) | copy-start | bytes 1572868
  159.6 373.5 %copy-start.2 = (bf16[512,512]{1,0:T(8,128)(2,1)S(1)}, bf16[512,512]{1,0:T(8,128)(2,1)}, u32[]{:S(2)}) copy-start(bf16[512,512]{1,0:T(8,128)(2,1)} %param.14) | copy-start | bytes 1572868
  226.8 302.9 %reduce-scatter.5.cloned.1.call-start = ((), (), s32[]{:S(2)}) async-start(), calls=%async_computation.4 | async-start | bytes 1114112 | tf_op jit(solution)/shard_map/reduce_scatter | solution.py:97
  327.9 468.4 %all-reduce.3.cloned.1.call-start = ((), (), s32[]{:S(2)}) async-start(), calls=%async_computation.5 | async-start | bytes 4194304 | tf_op jit(solution)/shard_map/psum | solution.py:104
Sparse Core Ops, SparseCore 0:
  10.4 57.5 all-gather.1
  226.9 100.9 reduce-scatter.2
  331.7 197.8 reduce-scatter.4
  535.6 260.6 all-reduce.2
where the time goes:
time: 811 us; the launch traced here: 808 us
  waiting for transfers between devices  620 us (76%)
  matrix products  63 us (8%)
  loops' own time  42.4 us (5%)
  other arithmetic  40.2 us (5%)
  local copies, waits for them, and re-layouts  27.9 us (3%)
  between operations  14.5 us (2%)
    psum x1, waiting for transfers between devices, local(): lax.psum((self_partial, message_partial), ('row', 'blk'))  262 us
    reduce_scatter x1, waiting for transfers between devices, local(): lax.psum_scatter(block_sum, 'row', scatter_dimension=0, tiled=True)  200 us
    reduce_scatter x1, waiting for transfers between devices, local(): lax.psum_scatter(lax.fori_loop(0, block_rows * lax.axis_size('blk') // ti...  101 us
    all_gather x1, waiting for transfers between devices, local(): pieces = lax.all_gather(projected, 'blk', axis=0, tiled=True)  56.8 us
    dot_general x16, matrix products, gather_visit(): jnp.einsum('trc,cw->trw', pattern, source_tile, preferred_element_type=jn...  25.9 us
    dot_general x16, matrix products, tile_terms(): jnp.einsum('trc,trw->tcw', pattern, grads, preferred_element_type=jnp.flo...  25.1 us
    another operation x1, loops' own time, local(): gathered = lax.fori_loop(0, piece_tiles, gather_visit, start_sum)  21.4 us
    another operation x1, loops' own time, local(): lax.fori_loop(0, block_rows * lax.axis_size('blk') // tile_rows, partial_...  21 us
  transfers between devices with their start and end apart: 4, of which 4 were waited for; matrix products, arithmetic and copies ran while one was open for 1% of the time, Pallas kernels for 0%

commit v1 on v0

--- a/solution.py
+++ b/solution.py
@@ -48,7 +48,10 @@
     slot_of = slot_table(tile_lists)
     offset_tiles = key_offsets.reshape(tiles_here, tile_rows, slot_count)
     start_sum = jnp.zeros((target_table.shape[0], width), jnp.float32)
-    pieces = lax.all_gather(projected, "blk", axis=0, tiled=True)
+    read_the_edge = lambda buf: jnp.concatenate(
+        lax.all_to_all(jnp.stack(lax.axis_size("blk") * [buf], axis=0), "blk", 0, 0), axis=0
+    )
+    pieces = read_the_edge(projected)
     piece_tiles = pieces.shape[0] // tile_rows
 
     def gather_visit(local_tile, running):

time: 811 us -> 877 us (1.081)
  waiting for transfers between devices: 620 us -> 691 us
  other arithmetic: 40.2 us -> 27.4 us
    all_to_all x0 -> x1, waiting for transfers between devices: none -> 120 us  [local(): lax.all_to_all(jnp.stack(lax.axis_size('blk') * [buf], axis=0), 'blk', 0, 0)]
    all_gather x1 -> x0, waiting for transfers between devices: 56.8 us -> none  [local(): pieces = lax.all_gather(projected, 'blk', axis=0, tiled=True)]
    reduce_sum x32, other arithmetic: 15 us -> 2.91 us  [tile_patterns(): chosen = jnp.sum(jnp.where(chosen_slot, offset_tiles, 0), axis=2)]
where the time goes in v1:
time: 877 us; the launch traced here: 875 us
  waiting for transfers between devices  691 us (79%)
  matrix products  60.9 us (7%)
  loops' own time  42.4 us (5%)
  local copies, waits for them, and re-layouts  31.9 us (4%)
  other arithmetic  27.4 us (3%)
  between operations  14.5 us (2%)
    psum x1, waiting for transfers between devices, local(): lax.psum((self_partial, message_partial), ('row', 'blk'))  262 us
    reduce_scatter x1, waiting for transfers between devices, local(): lax.psum_scatter(block_sum, 'row', scatter_dimension=0, tiled=True)  200 us
    all_to_all x1, waiting for transfers between devices, local(): lax.all_to_all(jnp.stack(lax.axis_size('blk') * [buf], axis=0), 'blk', 0, 0)  120 us
    reduce_scatter x1, waiting for transfers between devices, local(): lax.psum_scatter(lax.fori_loop(0, block_rows * lax.axis_size('blk') // ti...  109 us
    dot_general x16, matrix products, gather_visit(): jnp.einsum('trc,cw->trw', pattern, source_tile, preferred_element_type=jn...  25.9 us
    dot_general x16, matrix products, tile_terms(): jnp.einsum('trc,trw->tcw', pattern, grads, preferred_element_type=jnp.flo...  25.1 us
    another operation x1, loops' own time, local(): gathered = lax.fori_loop(0, piece_tiles, gather_visit, start_sum)  21.4 us
    another operation x1, loops' own time, local(): lax.fori_loop(0, block_rows * lax.axis_size('blk') // tile_rows, partial_...  20.9 us
  transfers between devices with their start and end apart: 4, of which 4 were waited for; matrix products, arithmetic and copies ran while one was open for 1% of the time, Pallas kernels for 0%

profile of v1, /device:TPU:2, one launch (start us, length us, event | category | flops | bytes accessed | tf_op | source)
XLA Modules:
  0.0 874.8 jit_solution(6938814341370827293)
XLA Ops:
  7.2 1.7 convolution_convert_fusion
  8.9 4.0 stack.2
  12.9 6.9 all-to-all-start
  20.7 120.3 %all-to-all-done = bf16[16,512,512]{2,1,0:T(8,128)(2,1)} async-done(((bf16[16,512,512]{2,1,0:T(8,128)(2,1)}), bf16[16,512,512]{2,1,0:T(8,128)(2,1)}, u32[]{:S(2)}, u32[]{:S(2)}) %all-to-all-start) | async-done | bytes 8388640 | tf_op jit(solution)/shard_map/all_to_all | solution.py:52
  141.0 68.5 %while.28 = (s32[]{:T(128)}, f32[512,512]{1,0:T(8,128)S(1)}, s32[1,16]{1,0:T(1,128)S(1)}, s32[1,512,16]{1,2,0:T(8,128)S(1)}, s32[1]{0:T(128)}, /*index=5*/bf16[8...) while((s32[]{:T(128)}, f32[512,512]{1,0:T(8,128)S(1)}, s32[1,16]{1,0:T(1,128)S(1)}, ...), condition=%wide.region_3.4_spmd.clone, body=%wide.region_1.3_spmd.clone.sunk | while | flops 269499936 | bytes 2659034 | solution.py:64
  143.6 1.6 convolution_add_fusion.4
  147.9 1.6 convolution_add_fusion.4
  152.2 1.6 convolution_add_fusion.4
  156.5 1.6 convolution_add_fusion.4
  160.8 1.6 convolution_add_fusion.4
  165.0 1.6 convolution_add_fusion.4
  169.3 1.6 convolution_add_fusion.4
  173.6 1.6 convolution_add_fusion.4
  177.9 1.6 convolution_add_fusion.4
  182.2 1.6 convolution_add_fusion.4
  186.5 1.6 convolution_add_fusion.4
  190.7 1.6 convolution_add_fusion.4
  195.0 1.6 convolution_add_fusion.4
  199.3 1.6 convolution_add_fusion.4
  203.6 1.6 convolution_add_fusion.4
  207.9 1.6 convolution_add_fusion.4
  209.5 1.7 fusion.15
  211.2 7.9 broadcast_in_dim.94
  219.1 67.1 %while.27 = (s32[]{:T(128)}, f32[8192,512]{1,0:T(8,128)}, s32[1,16]{1,0:T(1,128)S(1)}, s32[1,512,16]{1,2,0:T(8,128)S(1)}, s32[1]{0:T(128)}, /*index=5*/bf16[1,51...) while((s32[]{:T(128)}, f32[8192,512]{1,0:T(8,128)}, ...), condition=%wide.region_6.7_spmd, body=%wide.region_4.6_spmd.sunk | while | flops 269237792 | bytes 1610968 | solution.py:90
  255.3 1.6 fusion.37
  272.1 1.6 fusion.37
  286.3 108.5 %reduce-scatter.3.cloned.1.call-done = f32[512,512]{1,0:T(8,128)} async-done(((f32[8192,512]{1,0:T(8,128)}), f32[512,512]{1,0:T(8,128)}) %reduce-scatter.3.cloned.1.call-update) | async-done | bytes 1048592 | tf_op jit(solution)/shard_map/reduce_scatter | solution.py:89
  396.3 200.2 %reduce-scatter.5.cloned.1.call-done = f32[32,512]{1,0:T(8,128)} async-done(((f32[512,512]{1,0:T(8,128)}), f32[32,512]{1,0:T(8,128)}) %reduce-scatter.5.cloned.1.call-update) | async-done | bytes 65552 | tf_op jit(solution)/shard_map/reduce_scatter | solution.py:100
  596.5 2.1 fusion.16
  600.0 1.7 convolution_convert_fusion.1
  601.7 261.6 %all-reduce.3.cloned.1.call-done = (f32[512,512]{0,1:T(8,128)}, f32[512,512]{1,0:T(8,128)}) async-done(((f32[512,512]{0,1:T(8,128)}, f32[512,512]{1,0:T(8,128)}), (f32[512,512]{0,1:T(8,128)}, f32[512,512]{1,0:T(8,128)})) %all-reduce.3.cloned.1.call-update) | async-done | bytes 2097168 | tf_op jit(solution)/shard_map/psum | solution.py:107
  865.9 2.3 broadcast_multiply_fusion
  (134 shorter events, 69.8 us)
Async XLA Ops:
  7.2 202.4 %copy-start = (bf16[512,512]{1,0:T(8,128)(2,1)S(1)}, bf16[512,512]{1,0:T(8,128)(2,1)}, u32[]{:S(2)}) copy-start(bf16[512,512]{1,0:T(8,128)(2,1)} %param.15) | copy-start | bytes 1572868
  7.2 13.4 %copy-start.5 = (s32[1,16]{1,0:T(1,128)S(1)}, s32[1,16]{1,0:T(1,128)}, u32[]{:S(2)}) copy-start(s32[1,16]{1,0:T(1,128)} %param.16) | copy-start | bytes 196
  7.2 133.8 %copy-start.1 = (s32[512,16]{0,1:T(8,128)S(1)}, s32[512,16]{0,1:T(8,128)}, u32[]{:S(2)}) copy-start(s32[512,16]{0,1:T(8,128)} %param.17) | copy-start | bytes 98308
  12.9 196.6 %copy-start.3 = (bf16[512,512]{1,0:T(8,128)(2,1)S(1)}, bf16[512,512]{1,0:T(8,128)(2,1)}, u32[]{:S(2)}) copy-start(bf16[512,512]{1,0:T(8,128)(2,1)} %param.13) | copy-start | bytes 1572868
  12.9 196.6 %copy-start.4 = (bf16[512,512]{1,0:T(8,128)(2,1)S(1)}, bf16[512,512]{1,0:T(8,128)(2,1)}, u32[]{:S(2)}) copy-start(bf16[512,512]{1,0:T(8,128)(2,1)} %param.19) | copy-start | bytes 1572868
  12.9 128.1 %all-to-all-start = ((bf16[16,512,512]{2,1,0:T(8,128)(2,1)}), bf16[16,512,512]{2,1,0:T(8,128)(2,1)}, u32[]{:S(2)}, u32[]{:S(2)}) async-start(bf16[16,512,512]{2,1,0:T(8,128)(2,1)} %stack.2), calls=%async_computation | async-start | bytes 16777216 | tf_op jit(solution)/shard_map/all_to_all | solution.py:52
  19.9 374.9 %reduce-scatter.3.cloned.1.call-start = ((), (), s32[]{:S(2)}) async-start(), calls=%async_computation.3 | async-start | bytes 17825792 | tf_op jit(solution)/shard_map/reduce_scatter | solution.py:89
  219.1 380.9 %copy-start.2 = (bf16[512,512]{1,0:T(8,128)(2,1)S(1)}, bf16[512,512]{1,0:T(8,128)(2,1)}, u32[]{:S(2)}) copy-start(bf16[512,512]{1,0:T(8,128)(2,1)} %param.14) | copy-start | bytes 1572868
  286.2 310.3 %reduce-scatter.5.cloned.1.call-start = ((), (), s32[]{:S(2)}) async-start(), calls=%async_computation.4 | async-start | bytes 1114112 | tf_op jit(solution)/shard_map/reduce_scatter | solution.py:100
  394.8 468.5 %all-reduce.3.cloned.1.call-start = ((), (), s32[]{:S(2)}) async-start(), calls=%async_computation.5 | async-start | bytes 4194304 | tf_op jit(solution)/shard_map/psum | solution.py:107
Sparse Core Ops, SparseCore 0:
  286.4 108.3 reduce-scatter.2
  398.6 197.8 reduce-scatter.4
  602.7 260.5 all-reduce.2
